TPU v7x, 32 devices: a whole 2x2x4 slice. The times are simulated.
32 devices in a mesh: tok: 2 (over x), blk: 16 (over z, y, core).
Axes of the slice: x: 2, y: 2, z: 4, core: 2. Of those that a mesh axis runs over, the one named last changes fastest.
Arguments:
- hidden_in: bfloat16 [16, 256, 1024], P('blk', 'tok'), may hold values from -22 to 22
- seg_ids: int32 [16, 256], P('blk'), may hold values from 0 to 3, never falling along the last dimension, each value on 1 to 128 neighbouring positions
- norm_gain1: float32 [1024], replicated, may hold values from 0.1 to 1.9
- w_query: bfloat16 [1024, 1024], replicated, may hold values from -0.0234375 to 0.0234375
- w_key_value: bfloat16 [1024, 2048], replicated, may hold values from -0.1875 to 0.1875
- rel_bias: float32 [32, 16], replicated, may hold values from -3 to 300
- w_attn_out: bfloat16 [1024, 1024], replicated, may hold values from -0.1875 to 0.1875
- norm_gain2: float32 [1024], replicated, may hold values from 0.1 to 1.9
- w_in: bfloat16 [4096, 1024], P('blk'), may hold values from -0.1875 to 0.1875
- w_out: bfloat16 [4096, 1024], P('blk'), may hold values from -0.09375 to 0.09375
Outputs:
- layer_out: bfloat16 [16, 256, 1024], P('blk', 'tok')
Inputs may be any that keep to these rules, and one draw needn't show every extreme that they name: `seg_ids`: in each stream the segment numbers never fall; each of the 4 segments is a run of 1 to 128 tokens, one exactly 128 long.
All inputs are finite; a program needn't handle non-finite values.
Results may differ from a plain program's by a relative error of at most 0.007.
Values may be sent and summed in bfloat16 or wider, within the bound.
A program may use at most 192 MiB of HBM per device.

v0:
```python
import jax
import jax.numpy as jnp
from jax import lax
from jax.sharding import PartitionSpec as P

D = 1024
HEADS = 16
HD = 64


bucket_bounds = (12, 16, 23, 32, 46, 64, 91)
epsilon = 1e-06


def bucket_of(offset):
    distance = jnp.abs(offset)
    far_bucket = jnp.full_like(distance, 8)
    for boundary in bucket_bounds:
        far_bucket = far_bucket + (distance >= boundary).astype(jnp.int32)
    chosen = jnp.where(distance < 8, distance, far_bucket)
    return chosen + 16 * (offset > 0).astype(jnp.int32)


def rms_scale(values, gain):
    mean_square = jnp.mean(values * values, axis=-1, keepdims=True)
    return values * lax.rsqrt(mean_square + epsilon) * gain


def per_device(
    hidden_in,
    seg_ids,
    norm_gain1,
    w_query,
    w_key_value,
    rel_bias,
    w_attn_out,
    norm_gain2,
    w_in,
    w_out,
):
    tok_place = lax.axis_index("tok")
    rows_here = hidden_in.shape[1]
    hidden = hidden_in[0].astype(jnp.float32)
    normed = rms_scale(hidden, norm_gain1).astype(jnp.bfloat16)
    queries = (
        jnp.dot(normed, w_query, preferred_element_type=jnp.float32)
        .astype(jnp.bfloat16)
        .reshape(rows_here, HEADS, HD)
    )
    segment_row = seg_ids[0]
    query_pos = tok_place * rows_here + jnp.arange(rows_here, dtype=jnp.int32)
    query_seg = lax.dynamic_slice_in_dim(segment_row, tok_place * rows_here, rows_here)
    bias_table = jnp.transpose(rel_bias)
    keys_values = jnp.dot(normed, w_key_value, preferred_element_type=jnp.float32).astype(
        jnp.bfloat16
    )
    attend_keys_values = lax.all_gather(keys_values, "tok", axis=0, tiled=True)
    count = attend_keys_values.shape[0]
    old_max = jnp.full((HEADS, rows_here), -1e30, jnp.float32)
    key_heads = attend_keys_values[:, :D].reshape(count, HEADS, HD)
    value_heads = attend_keys_values[:, D:].reshape(count, HEADS, HD)
    offsets = jnp.arange(count, dtype=jnp.int32)[None, :] - query_pos[:, None]
    same_segment = (query_seg[:, None] == segment_row[None, :])[None]
    bias_block = jnp.where(same_segment, jnp.take(bias_table, bucket_of(offsets), axis=1), -1e30)
    masked = (
        jnp.einsum("qhd,khd->hqk", queries, key_heads, preferred_element_type=jnp.float32)
        + bias_block
    )
    new_max = jnp.maximum(old_max, jnp.max(masked, axis=-1))
    exps = jnp.where(same_segment, jnp.exp(masked - new_max[..., None]), 0.0)
    new_sum = jnp.sum(exps, axis=-1)
    new_acc = jnp.einsum(
        "hqk,khd->hqd", exps.astype(jnp.bfloat16), value_heads, preferred_element_type=jnp.float32
    )
    mixed = new_acc / new_sum[..., None]
    attended = jnp.transpose(mixed, (1, 0, 2)).reshape(rows_here, D).astype(jnp.bfloat16)
    middle = hidden + jnp.dot(attended, w_attn_out, preferred_element_type=jnp.float32)
    normed_two = rms_scale(middle, norm_gain2).astype(jnp.bfloat16)
    inner = jax.nn.relu(
        lax.dot_general(
            lax.all_gather(normed_two, "blk", axis=0, tiled=True),
            w_in,
            (((1,), (1,)), ((), ())),
            preferred_element_type=jnp.float32,
        )
    ).astype(jnp.bfloat16)
    terms = (
        jnp.dot(inner, w_out, preferred_element_type=jnp.float32)
        .astype(jnp.bfloat16)
        .astype(jnp.float32)
    )
    feed = lax.psum_scatter(
        terms.astype(jnp.bfloat16), "blk", scatter_dimension=0, tiled=True
    ).astype(jnp.float32)
    return (middle + feed).astype(jnp.bfloat16)[None]


def solution(mesh):
    placed = (
        P("blk", "tok", None),
        P("blk", None),
        P(),
        P(),
        P(),
        P(),
        P(),
        P(),
        P("blk", None),
        P("blk", None),
    )
    return jax.shard_map(
        per_device, mesh=mesh, in_specs=placed, out_specs=P("blk", "tok", None), check_vma=False
    )
```

profile of v0, /device:TPU:0, one launch (start us, length us, event | category | flops | bytes accessed | tf_op | source)
XLA Modules:
  0.0 288.1 jit_solution(8687728159176123774)
XLA Ops:
  6.5 0.0 copy-start
  6.5 1.2 fusion.10
  7.8 3.9 %convolution_convert_fusion.1 = bf16[128,2048]{1,0:T(8,128)(2,1)} fusion(bf16[1024,2048]{1,0:T(8,128)(2,1)} %param.14, bf16[1,128,1024]{2,1,0:T(8,128)(2,1)} %param.10, f32[1024]{0:T(1024)} %param.12, f32[128]{0:T(128)S(1)} %add_rsqrt_fusion.1), kind=kOutput, calls=%fused_computation.4 | convolution fusion | flops 537657344 | bytes 4985344 | tf_op jit(solution)/shard_map/dot_general | solution.py:54
  11.7 0.0 all-gather.3.cloned.1.call-update
  11.7 0.0 all-gather.5.cloned.1.call-start
  11.8 0.2 fusion.16
  12.0 0.1 copy.22
  12.1 0.0 copy-done.4
  12.1 0.1 copy.18
  12.2 108.5 %gather_fusion = f32[32768,16]{1,0:T(8,128)} fusion(f32[16,32]{0,1:T(8,128)S(1)} %bitcast.41, s32[32768]{0:T(1024)S(1)} %broadcast_clamp_fusion), kind=kCustom, calls=%fused_computation | custom fusion | bytes 4325376 | tf_op jit(solution)/shard_map/jit(_take)/gather | solution.py:64
  120.6 11.1 %copy.21 = f32[128,256,16]{1,0,2:T(8,128)} copy(f32[128,256,16]{2,1,0:T(8,128)} %bitcast.42) | data formatting | bytes 4194304 | tf_op jit(solution)/shard_map/jit(_take)/gather | solution.py:64
  131.7 2.1 convolution_convert_fusion.2
  133.8 0.8 copy.16
  134.7 0.3 compare_and_fusion
  134.9 0.0 all-gather.3.cloned.1.call-done
  134.9 2.1 fusion.39
  137.0 1.2 copy.17
  138.3 3.6 %fusion.40 = (f32[16,128]{1,0:T(8,128)S(1)}, f32[16,128,256]{2,1,0:T(8,128)}) fusion(f32[128,256,16]{1,0,2:T(8,128)} %copy.21, pred[128,256]{1,0:T(8,128)(4,1)S(1)} %get-tuple-element.11, pred[128,256]{1,0:T(8,128)(4,1)S(1)} %get-tuple-element.12, bf16[128,16,64]{0,2,1:T(8,128)(2,1)} %bitcast.44, bf16[256,16,64]{0,2,1:T(8,128)(2,1)S(1)} %bitcast.43), kind=kOutput, calls=%fused_computation.65 | convolution fusion | flops 69203968 | bytes 5054464 | tf_op jit(solution)/shard_map/qhd,khd->hqk/dot_general | solution.py:66
  141.9 0.2 copy.20
  142.1 2.4 fusion.1
  144.5 0.6 fusion.4
  145.1 0.0 copy-start.5
  145.1 0.5 multiply_reduce_fusion
  145.7 0.1 copy-done.5
  145.8 0.8 multiply_convert_fusion
  146.6 0.0 all-gather.5.cloned.1.call-update
  146.6 0.0 reduce-scatter.2.cloned.1.call-start
  146.7 53.4 %all-gather.5.cloned.1.call-done = bf16[2048,1024]{1,0:T(8,128)(2,1)} async-done(((bf16[128,1024]{1,0:T(8,128)(2,1)}), bf16[2048,1024]{1,0:T(8,128)(2,1)}) %all-gather.5.cloned.1.call-update) | async-done | bytes 4194320 | tf_op jit(solution)/shard_map/all_gather | solution.py:81
  200.1 8.5 %convolution_convert_fusion = bf16[2048,1024]{1,0:T(8,128)(2,1)} fusion(bf16[256,1024]{1,0:T(8,128)(2,1)} %param.19, bf16[2048,1024]{1,0:T(8,128)(2,1)} %all-gather.5.cloned.1.call-done, bf16[256,1024]{1,0:T(8,128)(2,1)} %param.18), kind=kOutput, calls=%fused_computation.1 | convolution fusion | flops 2150629376 | bytes 9437184 | tf_op jit(solution)/shard_map/dot_general | solution.py:88
  208.6 0.0 reduce-scatter.2.cloned.1.call-update
  208.6 71.3 %reduce-scatter.2.cloned.1.call-done = bf16[128,1024]{1,0:T(8,128)(2,1)} async-done(((bf16[2048,1024]{1,0:T(8,128)(2,1)}), bf16[128,1024]{1,0:T(8,128)(2,1)}) %reduce-scatter.2.cloned.1.call-update) | async-done | bytes 262160 | tf_op jit(solution)/shard_map/reduce_scatter | solution.py:92
  279.9 1.7 fusion.13
  (17 shorter events, 0.1 us)
Async XLA Ops:
  6.5 138.6 %copy-start = (bf16[1024,1024]{1,0:T(8,128)(2,1)S(1)}, bf16[1024,1024]{1,0:T(8,128)(2,1)}, u32[]{:S(2)}) copy-start(bf16[1024,1024]{1,0:T(8,128)(2,1)} %param.16) | copy-start | bytes 6291460
  6.5 128.4 %all-gather.3.cloned.1.call-start = ((), (), s32[]{:S(2)}) async-start(), calls=%async_computation.1 | async-start | bytes 1572864 | tf_op jit(solution)/shard_map/all_gather | solution.py:57
  7.8 4.3 %copy-start.4 = (f32[32,16]{0,1:T(8,128)S(1)}, f32[32,16]{0,1:T(8,128)}, u32[]{:S(2)}) copy-start(f32[32,16]{0,1:T(8,128)} %param.15) | copy-start | bytes 6148
  11.7 188.4 %all-gather.5.cloned.1.call-start = ((), (), s32[]{:S(2)}) async-start(), calls=%async_computation.2 | async-start | bytes 4456448 | tf_op jit(solution)/shard_map/all_gather | solution.py:81
  120.6 11.1 %copy-start.2 = (bf16[1,128,1024]{2,1,0:T(8,128)(2,1)S(1)}, bf16[1,128,1024]{2,1,0:T(8,128)(2,1)}, u32[]{:S(2)}) copy-start(bf16[1,128,1024]{2,1,0:T(8,128)(2,1)} %param.10) | copy-start | bytes 786436
  120.6 11.1 %copy-start.3 = (f32[1024]{0:T(1024)S(1)}, f32[1024]{0:T(1024)}, u32[]{:S(2)}) copy-start(f32[1024]{0:T(1024)} %param.12) | copy-start | bytes 12292
  131.7 2.9 %copy-start.6 = (s32[1,256]{1,0:T(1,128)S(1)}, s32[1,256]{1,0:T(1,128)}, u32[]{:S(2)}) copy-start(s32[1,256]{1,0:T(1,128)} %param.11) | copy-start | bytes 3076
  142.1 2.4 copy-start.1
  145.1 0.7 copy-start.5
  146.6 133.2 %reduce-scatter.2.cloned.1.call-start = ((), (), s32[]{:S(2)}) async-start(), calls=%async_computation.3 | async-start | bytes 4456448 | tf_op jit(solution)/shard_map/reduce_scatter | solution.py:92
Sparse Core Ops, SparseCore 0:
  11.8 23.9 all-gather.2
  146.8 53.2 all-gather.4
  208.7 71.0 reduce-scatter.1
where the time goes:
time: 289 us; the launch traced here: 288 us
  waiting for transfers between devices  125 us (43%)
  local copies, waits for them, and re-layouts  124 us (43%)
  matrix products  19.2 us (7%)
  between operations  13.2 us (5%)
  other arithmetic  6.67 us (2%)
    gather x2, local copies, waits for them, and re-layouts, per_device(): jnp.take(bias_table, bucket_of(offsets), axis=1)  120 us
    reduce_scatter x1, waiting for transfers between devices, per_device(): lax.psum_scatter(terms.astype(jnp.bfloat16), 'blk', scatter_dimension=0,...  71.3 us
    all_gather x1, waiting for transfers between devices, per_device(): lax.all_gather(normed_two, 'blk', axis=0, tiled=True)  53.4 us
    dot_general x1, matrix products, per_device(): jnp.dot(inner, w_out, preferred_element_type=jnp.float32)  8.51 us
  transfers between devices with their start and end apart: 3, of which 2 were waited for; matrix products, arithmetic and copies ran while one was open for 43% of the time, Pallas kernels for 0%

commit v1 on v0

v1 whole, which is shorter than its diff:
```python
import functools

import jax
import jax.numpy as jnp
from jax import lax
from jax.experimental import pallas as pl
from jax.experimental.pallas import tpu as pltpu
from jax.sharding import PartitionSpec as P

D = 1024
HEADS = 16
HD = 64
BUCKETS = 32

bucket_bounds = (12, 16, 23, 32, 46, 64, 91)
epsilon = 1e-06
MESH = pl.DeviceIdType.MESH
VM = pl.BlockSpec(memory_space=pltpu.VMEM)


def bucket_of(offset):
    distance = jnp.abs(offset)
    far_bucket = jnp.full_like(distance, 8)
    for boundary in bucket_bounds:
        far_bucket = far_bucket + (distance >= boundary).astype(jnp.int32)
    chosen = jnp.where(distance < 8, distance, far_bucket)
    return chosen + 16 * (offset > 0).astype(jnp.int32)


def rms_scale(values, gain):
    mean_square = jnp.mean(values * values, axis=-1, keepdims=True)
    return values * lax.rsqrt(mean_square + epsilon) * gain


def exchange_kernel(n_tok, x_ref, o_ref, send_sem, recv_sem, own_sem):
    me = lax.axis_index("tok")
    barrier = pltpu.get_barrier_semaphore()
    for d in range(1, n_tok):
        pl.semaphore_signal(
            barrier, inc=1, device_id={"tok": lax.rem(me + d, n_tok)}, device_id_type=MESH
        )
    own = pltpu.make_async_copy(x_ref, o_ref.at[me], own_sem)
    own.start()
    pl.semaphore_wait(barrier, n_tok - 1)
    copies = []
    for d in range(1, n_tok):
        copy = pltpu.make_async_remote_copy(
            src_ref=x_ref,
            dst_ref=o_ref.at[me],
            send_sem=send_sem.at[d],
            recv_sem=recv_sem.at[d],
            device_id={"tok": lax.rem(me + d, n_tok)},
            device_id_type=MESH,
        )
        copy.start()
        copies.append(copy)
    own.wait()
    for copy in copies:
        copy.wait()


def exchange(x, n_tok):
    rows = x.shape[0]
    return pl.pallas_call(
        functools.partial(exchange_kernel, n_tok),
        out_shape=jax.ShapeDtypeStruct((n_tok, rows, D), jnp.bfloat16),
        in_specs=[VM],
        out_specs=VM,
        scratch_shapes=[
            pltpu.SemaphoreType.DMA((n_tok,)),
            pltpu.SemaphoreType.DMA((n_tok,)),
            pltpu.SemaphoreType.DMA,
        ],
        compiler_params=pltpu.CompilerParams(collective_id=0, has_side_effects=True),
    )(x)


def attention_kernel(
    hid_ref, seg_row_ref, seg_col_ref, g1_ref, wq_ref, wkv_ref, bias_ref, wo_ref, g2_ref,
    mid_ref, n2_ref, q_scr, kv_scr, att_scr,
):
    tok = lax.axis_index("tok")
    n_tok, rows, _ = hid_ref.shape
    count = n_tok * rows
    wide = 2 * count
    for part in range(n_tok):
        normed = rms_scale(hid_ref[part].astype(jnp.float32), g1_ref[...]).astype(jnp.bfloat16)
        kv_scr[part * rows:(part + 1) * rows, :] = jnp.dot(
            normed, wkv_ref[...], preferred_element_type=jnp.float32
        ).astype(jnp.bfloat16)
    hidden = hid_ref[tok].astype(jnp.float32)
    normed = rms_scale(hidden, g1_ref[...]).astype(jnp.bfloat16)
    q_scr[...] = jnp.dot(normed, wq_ref[...], preferred_element_type=jnp.float32).astype(
        jnp.bfloat16
    )
    spot = lax.broadcasted_iota(jnp.int32, (BUCKETS, wide), 1)
    offset = jnp.where(spot < count, spot, spot - wide) - tok * rows
    chosen = lax.broadcasted_iota(jnp.int32, (BUCKETS, wide), 0) == bucket_of(offset)
    bias_line = jnp.dot(
        bias_ref[...], chosen.astype(jnp.float32),
        precision=lax.Precision.HIGHEST, preferred_element_type=jnp.float32,
    )
    same = seg_col_ref[...] == seg_row_ref[...]
    lane = lax.broadcasted_iota(jnp.int32, (rows, 2 * HD), 1)
    low = lane < HD
    for pair in range(HEADS // 2):
        at = pair * 2 * HD
        q_two = q_scr[:, at:at + 2 * HD]
        k_two = kv_scr[:, at:at + 2 * HD]
        v_two = kv_scr[:, D + at:D + at + 2 * HD]
        halves = []
        for half in range(2):
            head = 2 * pair + half
            keep = low if half == 0 else jnp.logical_not(low)
            q_one = jnp.where(keep, q_two, jnp.zeros_like(q_two))
            scores = lax.dot_general(
                q_one, k_two, (((1,), (1,)), ((), ())), preferred_element_type=jnp.float32
            )
            line = jnp.broadcast_to(bias_line[head:head + 1, :], (rows, wide))
            bias = pltpu.roll(line, 0, 1, stride=1, stride_axis=0)[:, :count]
            masked = jnp.where(same, scores + bias, -1e30)
            top = jnp.max(masked, axis=-1, keepdims=True)
            exps = jnp.exp(masked - top)
            total = jnp.sum(exps, axis=-1, keepdims=True)
            mixed = jnp.dot(exps.astype(jnp.bfloat16), v_two, preferred_element_type=jnp.float32)
            halves.append(mixed / total)
        att_scr[:, at:at + 2 * HD] = jnp.where(low, halves[0], halves[1]).astype(jnp.bfloat16)
    middle = hidden + jnp.dot(att_scr[...], wo_ref[...], preferred_element_type=jnp.float32)
    mid_ref[...] = middle
    n2_ref[...] = rms_scale(middle, g2_ref[...]).astype(jnp.bfloat16)


def attention(hid, seg_row, seg_col, g1, wq, wkv, bias_t, wo, g2):
    n_tok, rows, _ = hid.shape
    return pl.pallas_call(
        attention_kernel,
        out_shape=(
            jax.ShapeDtypeStruct((rows, D), jnp.float32),
            jax.ShapeDtypeStruct((rows, D), jnp.bfloat16),
        ),
        in_specs=[VM] * 9,
        out_specs=(VM, VM),
        scratch_shapes=[
            pltpu.VMEM((rows, D), jnp.bfloat16),
            pltpu.VMEM((n_tok * rows, 2 * D), jnp.bfloat16),
            pltpu.VMEM((rows, D), jnp.bfloat16),
        ],
        compiler_params=pltpu.CompilerParams(vmem_limit_bytes=48 << 20),
    )(hid, seg_row, seg_col, g1, wq, wkv, bias_t, wo, g2)


def mlp_kernel(
    DEEP, WIDE, n2_ref, win_ref, wout_ref, mid_ref, out_ref,
    gath, part, cross, side_in, chain_in, acc,
    s_chain, s_side, s_core, r_gath, s_cross, r_cross, s_ret, r_ret, s_sum, r_sum,
):
    blk = lax.axis_index("blk")
    c = lax.rem(blk, 2)
    chip = blk // 2
    y = lax.rem(chip, WIDE)
    z = chip // WIDE
    rows = n2_ref.shape[0]
    oc = 1 - c

    def dev(zz, yy, cc):
        return {"blk": (zz * WIDE + yy) * 2 + cc}

    def remote(src, dst, ss, rs, to):
        return pltpu.make_async_remote_copy(
            src_ref=src, dst_ref=dst, send_sem=ss, recv_sem=rs, device_id=to, device_id_type=MESH
        )

    has_up = z < DEEP - 1
    has_down = z > 0

    barrier = pltpu.get_barrier_semaphore()
    pl.semaphore_signal(barrier, inc=1, device_id=dev(z, y, oc), device_id_type=MESH)
    for d in range(1, WIDE):
        pl.semaphore_signal(
            barrier, inc=1, device_id=dev(z, lax.rem(y + d, WIDE), c), device_id_type=MESH
        )

    @pl.when(has_up)
    def _():
        pl.semaphore_signal(barrier, inc=1, device_id=dev(z + 1, y, c), device_id_type=MESH)

    @pl.when(has_down)
    def _():
        pl.semaphore_signal(barrier, inc=1, device_id=dev(z - 1, y, c), device_id_type=MESH)

    gath[chip, c] = n2_ref[...]
    ends = jnp.where(has_up, 1, 0) + jnp.where(has_down, 1, 0)
    pl.semaphore_wait(barrier, WIDE + ends)

    def pass_on(i, core, to, ss):
        return remote(gath.at[i, core], gath.at[i, core], ss, r_gath.at[i, core], to)

    def arrived(i, core):
        pass_on(i, core, dev(z, y, oc), s_core.at[i]).wait_recv()

    def up(i):
        return pass_on(i, c, dev(z + 1, y, c), s_chain.at[0, i // WIDE])

    def down(i):
        return pass_on(i, c, dev(z - 1, y, c), s_chain.at[1, i // WIDE])

    def side(i, d):
        return pass_on(i, c, dev(z, lax.rem(y + d, WIDE), c), s_side.at[d, i // WIDE])

    def core(i):
        return pass_on(i, c, dev(z, y, oc), s_core.at[i])

    sense = 1 - 2 * lax.rem(z, 2)
    if DEEP == 4:
        inner_place = lax.rem((z + 1) // 2, 2)
        reach = [sense * (j * (1 - inner_place) + (0, 1, -1, -2)[j] * inner_place) for j in range(4)]
        order = [z + r for r in reach]
    else:
        order = [lax.rem(z + j, DEEP) for j in range(DEEP)]

    def stage_column(j):
        zz = order[j]
        i = zz * WIDE + y
        if j > 0:
            arrived(i, c)

            @pl.when(jnp.logical_and(zz < z, has_up))
            def _():
                up(i).start()

            @pl.when(jnp.logical_and(zz > z, has_down))
            def _():
                down(i).start()
        else:

            @pl.when(has_up)
            def _():
                up(i).start()

            @pl.when(has_down)
            def _():
                down(i).start()
        for d in range(1, WIDE):
            side(i, d).start()
        core(i).start()

    def stage_side(j):
        for d in range(1, WIDE):
            i = order[j] * WIDE + lax.rem(y + d, WIDE)
            arrived(i, c)
            core(i).start()

    def cross_copy(i):
        return remote(part.at[i, oc], cross.at[i], s_cross.at[i], r_cross.at[i], dev(z, y, oc))

    def stage_compute(j):
        def one(d, carry):
            i = order[j] * WIDE + lax.rem(y + d, WIDE)
            arrived(i, oc)
            tokens = gath[i].reshape(2 * rows, D)
            hidden = lax.dot_general(
                tokens, win_ref[...], (((1,), (1,)), ((), ())), preferred_element_type=jnp.float32
            )
            hidden = jnp.maximum(hidden, 0.0).astype(jnp.bfloat16)
            terms = jnp.dot(hidden, wout_ref[...], preferred_element_type=jnp.float32)
            part[i] = terms.astype(jnp.bfloat16).reshape(2, rows, D)
            cross_copy(i).start()
            return carry

        lax.fori_loop(1, WIDE + 1, one, 0)

    def both_cores(i):
        cross_copy(i).wait_recv()
        return part[i, c].astype(jnp.float32) + cross[i].astype(jnp.float32)

    def ret_copy(j, d):
        i = order[j] * WIDE + lax.rem(y + d, WIDE)
        return remote(
            part.at[i, c], side_in.at[d - 1, order[j]],
            s_ret.at[d - 1, order[j]], r_ret.at[d - 1, order[j]],
            dev(z, lax.rem(y + d, WIDE), c),
        )

    def stage_return(j):
        for d in range(1, WIDE):
            i = order[j] * WIDE + lax.rem(y + d, WIDE)
            part[i, c] = both_cores(i).astype(jnp.bfloat16)
            ret_copy(j, d).start()

    def column_sum(j):
        total = both_cores(order[j] * WIDE + y)
        for d in range(1, WIDE):
            ret_copy(j, d).wait_recv()
            total = total + side_in[d - 1, order[j]].astype(jnp.float32)
        return total

    def sum_up(target):
        return remote(
            part.at[target * WIDE + y, c], chain_in.at[target],
            s_sum.at[target], r_sum.at[target], dev(z + 1, y, c),
        )

    def sum_down(target):
        slot = jnp.where(target == z - 1, DEEP, target)
        return remote(
            part.at[target * WIDE + y, c], chain_in.at[slot],
            s_sum.at[target], r_sum.at[slot], dev(z - 1, y, c),
        )

    def sum_arrived(slot):
        remote(
            chain_in.at[slot], chain_in.at[slot], s_sum.at[0], r_sum.at[slot], dev(z, y, oc)
        ).wait_recv()
        return chain_in[slot].astype(jnp.float32)

    stage_column(0)
    for j in range(DEEP):
        if j + 1 < DEEP:
            stage_column(j + 1)
        stage_side(j)
        stage_compute(j)
        if j > 0:
            stage_return(j - 1)
    stage_return(DEEP - 1)

    for j in range(DEEP - 1, 0, -1):
        target = order[j]
        i = target * WIDE + y
        acc[...] = column_sum(j)
        upward = target > z

        @pl.when(jnp.where(upward, has_down, has_up))
        def _():
            acc[...] += sum_arrived(target)

        part[i, c] = acc[...].astype(jnp.bfloat16)

        @pl.when(upward)
        def _():
            sum_up(target).start()

        @pl.when(jnp.logical_not(upward))
        def _():
            sum_down(target).start()

    acc[...] = mid_ref[...] + column_sum(0)

    @pl.when(has_down)
    def _():
        acc[...] += sum_arrived(z)

    @pl.when(has_up)
    def _():
        acc[...] += sum_arrived(DEEP)

    out_ref[...] = acc[...].astype(jnp.bfloat16)

    for j in range(DEEP):
        i = order[j] * WIDE + y
        goes_up = has_up if j == 0 else jnp.logical_and(order[j] < z, has_up)
        goes_down = has_down if j == 0 else jnp.logical_and(order[j] > z, has_down)

        @pl.when(goes_up)
        def _():
            up(i).wait_send()

        @pl.when(goes_down)
        def _():
            down(i).wait_send()

        for d in range(1, WIDE):
            side(i, d).wait_send()
            ret_copy(j, d).wait_send()
        for d in range(WIDE):
            k = order[j] * WIDE + lax.rem(y + d, WIDE)
            core(k).wait_send()
            cross_copy(k).wait_send()
        if j > 0:

            @pl.when(order[j] > z)
            def _():
                sum_up(order[j]).wait_send()

            @pl.when(order[j] < z)
            def _():
                sum_down(order[j]).wait_send()


def mlp(n2, w_in, w_out, middle, n_blk):
    rows = n2.shape[0]
    deep = 4
    wide = n_blk // (2 * deep)
    chips = deep * wide
    spread = max(wide - 1, 1)
    dma = pltpu.SemaphoreType.DMA
    return pl.pallas_call(
        functools.partial(mlp_kernel, deep, wide),
        out_shape=jax.ShapeDtypeStruct((rows, D), jnp.bfloat16),
        in_specs=[VM] * 4,
        out_specs=VM,
        scratch_shapes=[
            pltpu.VMEM((chips, 2, rows, D), jnp.bfloat16),
            pltpu.VMEM((chips, 2, rows, D), jnp.bfloat16),
            pltpu.VMEM((chips, rows, D), jnp.bfloat16),
            pltpu.VMEM((spread, deep, rows, D), jnp.bfloat16),
            pltpu.VMEM((deep + 1, rows, D), jnp.bfloat16),
            pltpu.VMEM((rows, D), jnp.float32),
            dma((2, deep)),
            dma((wide, deep)),
            dma((chips,)),
            dma((chips, 2)),
            dma((chips,)),
            dma((chips,)),
            dma((spread, deep)),
            dma((spread, deep)),
            dma((deep + 1,)),
            dma((deep + 1,)),
        ],
        compiler_params=pltpu.CompilerParams(
            collective_id=1, has_side_effects=True, vmem_limit_bytes=60 << 20
        ),
    )(n2, w_in, w_out, middle)


def per_device(
    n_tok, n_blk, hidden_in, seg_ids, norm_gain1, w_query, w_key_value, rel_bias, w_attn_out,
    norm_gain2, w_in, w_out,
):
    hid = exchange(hidden_in[0], n_tok)
    rows = hidden_in.shape[1]
    seg_row = seg_ids
    start = lax.axis_index("tok") * rows
    seg_col = lax.dynamic_slice_in_dim(seg_ids[0], start, rows)[:, None]
    middle, n2 = attention(
        hid, seg_row, seg_col, norm_gain1[None], w_query, w_key_value, jnp.transpose(rel_bias),
        w_attn_out, norm_gain2[None],
    )
    return mlp(n2, w_in, w_out, middle, n_blk)[None]


def solution(mesh):
    placed = (
        P("blk", "tok", None),
        P("blk", None),
        P(),
        P(),
        P(),
        P(),
        P(),
        P(),
        P("blk", None),
        P("blk", None),
    )
    return jax.shard_map(
        functools.partial(per_device, mesh.shape["tok"], mesh.shape["blk"]),
        mesh=mesh, in_specs=placed, out_specs=P("blk", "tok", None), check_vma=False,
    )
```

time: 289 us -> 110 us (0.38)
  waiting for transfers between devices: 125 us -> 0 us
  local copies, waits for them, and re-layouts: 124 us -> 10.9 us
  Pallas kernels: 0 us -> 98.3 us
  matrix products: 19.2 us -> 0 us
  between operations: 13.2 us -> 0.05 us
  other arithmetic: 6.67 us -> 0 us
    gather x2 -> x0, local copies, waits for them, and re-layouts: 120 us -> none  [per_device(): jnp.take(bias_table, bucket_of(offsets), axis=1)]
    pallas_call x0 -> x3, Pallas kernels: none -> 98.3 us  [the longest x1 80.6 us: mlp(): pl.pallas_call(functools.partial(mlp_kernel, deep, wide), out_shape=jax.S...]
    reduce_scatter x1 -> x0, waiting for transfers between devices: 71.3 us -> none  [per_device(): lax.psum_scatter(terms.astype(jnp.bfloat16), 'blk', scatter_dimension=0,...]
    all_gather x2 -> x0, waiting for transfers between devices: 53.4 us -> none  [the longest x1 53.4 us: per_device(): lax.all_gather(normed_two, 'blk', axis=0, tiled=True)]
    dot_general x6 -> x0, matrix products: 19.2 us -> none  [the longest x1 8.51 us: per_device(): jnp.dot(inner, w_out, preferred_element_type=jnp.float32)]
    unnamed x16 -> x19, local copies, waits for them, and re-layouts: 0.28 us -> 10.1 us
    reduce_sum x2 -> x0, other arithmetic: 3.64 us -> none  [the longest x1 2.41 us: per_device(): new_sum = jnp.sum(exps, axis=-1)]
    slice x3 -> x0, local copies, waits for them, and re-layouts: 3.5 us -> none  [the longest x2 3.3 us: per_device(): key_heads = attend_keys_values[:, :D].reshape(count, HEADS, HD)]
  transfers between devices with their start and end apart: 3 -> 0, of which waited for: 2 -> 0; matrix products, arithmetic and copies ran while one was open for 43% -> 0% of each run, Pallas kernels for 0% -> 0%
where the time goes in v1:
time: 110 us; the launch traced here: 109 us
  Pallas kernels  98.3 us (89%)
  local copies, waits for them, and re-layouts  10.9 us (10%)
    pallas_call x1, Pallas kernels, mlp(): pl.pallas_call(functools.partial(mlp_kernel, deep, wide), out_shape=jax.S...  80.6 us
    pallas_call x1, Pallas kernels, exchange(): pl.pallas_call(functools.partial(exchange_kernel, n_tok), out_shape=jax.S...  11.1 us
    unnamed x19, local copies, waits for them, and re-layouts  10.1 us
    pallas_call x1, Pallas kernels, attention(): pl.pallas_call(attention_kernel, out_shape=(jax.ShapeDtypeStruct((rows, D...  6.65 us

profile of v1, /device:TPU:0, one launch (start us, length us, event | category | flops | bytes accessed | tf_op | source)
XLA Modules:
  0.0 109.2 jit_solution(13435074087308117822)
XLA Ops:
  0.0 0.7 dynamic-slice_bitcast_fusion
  0.7 0.1 copy.11.seg_col_ref
  0.8 11.1 %shard_map.100.hid_ref = bf16[2,128,1024]{2,1,0:T(8,128)(2,1)} custom-call(bf16[128,1024]{1,0:T(8,128)(2,1)} %bitcast.11), custom_call_target="tpu_custom_call" | custom-call | tf_op jit(solution)/shard_map/pallas_call | solution.py:64
  11.8 0.0 copy-start
  11.9 1.6 %copy-done = bf16[1024,1024]{1,0:T(8,128)(2,1)S(1)} copy-done((bf16[1024,1024]{1,0:T(8,128)(2,1)S(1)}, bf16[1024,1024]{1,0:T(8,128)(2,1)}, u32[]{:S(2)}) %copy-start) | copy-done | bytes 2097176
  13.4 0.0 copy-start.1
  13.4 1.6 %copy-done.1 = bf16[1024,1024]{1,0:T(8,128)(2,1)S(1)} copy-done((bf16[1024,1024]{1,0:T(8,128)(2,1)S(1)}, bf16[1024,1024]{1,0:T(8,128)(2,1)}, u32[]{:S(2)}) %copy-start.1) | copy-done | bytes 2097176
  15.0 0.0 copy-start.2
  15.0 1.0 copy-done.2
  16.1 0.0 copy-start.5
  16.1 0.7 copy-done.5
  16.8 0.0 copy-start.6
  16.8 0.7 copy-done.6
  17.5 0.0 copy-start.7
  17.5 0.7 copy-done.7
  18.1 0.0 copy-start.8
  18.1 0.7 copy-done.8
  18.8 6.6 %shard_map.101 = (f32[128,1024]{1,0:T(8,128)S(1)}, bf16[128,1024]{1,0:T(8,128)(2,1)S(1)}) custom-call(bf16[2,128,1024]{2,1,0:T(8,128)(2,1)S(1)} %copy-done.2, s32[1,256]{1,0:T(1,128)S(1)} %copy-done.8, s32[128,1]{1,0:T(8,128)S(1)} %copy.11.seg_col_ref, f32[1,1024]{1,0:T(1,128)S(1)} %bitcast.8, bf16[1024,1024]{1,0:T(8,128)(2,1)S(1)} %copy-done, ...), custom_call_target="tpu_custom_call" | custom-call | tf_op jit(solution)/shard_map/pallas_call | solution.py:135
  25.5 0.0 copy-start.3
  25.5 0.8 copy-done.3
  26.3 0.0 copy-start.4
  26.3 0.7 copy-done.4
  27.0 80.6 %shard_map.102 = bf16[128,1024]{1,0:T(8,128)(2,1)} custom-call(bf16[128,1024]{1,0:T(8,128)(2,1)} %copy-done.4, bf16[256,1024]{1,0:T(8,128)(2,1)} %win_ref.1, bf16[256,1024]{1,0:T(8,128)(2,1)} %wout_ref.1, f32[128,1024]{1,0:T(8,128)} %copy-done.3), custom_call_target="tpu_custom_call" | custom-call | tf_op jit(solution)/shard_map/pallas_call | solution.py:396
  107.6 1.7 %copy.13 = bf16[1,128,1024]{2,1,0:T(8,128)(2,1)} copy(bf16[1,128,1024]{2,1,0:T(8,128)(2,1)} %bitcast.10) | data formatting | bytes 524288
Async XLA Ops:
  11.8 1.6 %copy-start = (bf16[1024,1024]{1,0:T(8,128)(2,1)S(1)}, bf16[1024,1024]{1,0:T(8,128)(2,1)}, u32[]{:S(2)}) copy-start(bf16[1024,1024]{1,0:T(8,128)(2,1)} %wq_ref.1) | copy-start | bytes 6291460
  13.4 1.6 %copy-start.1 = (bf16[1024,1024]{1,0:T(8,128)(2,1)S(1)}, bf16[1024,1024]{1,0:T(8,128)(2,1)}, u32[]{:S(2)}) copy-start(bf16[1024,1024]{1,0:T(8,128)(2,1)} %wo_ref.1) | copy-start | bytes 6291460
  15.0 1.0 copy-start.2
  16.1 0.7 copy-start.5
  16.8 0.7 copy-start.6
  17.5 0.7 copy-start.7
  18.1 0.7 copy-start.8
  25.5 0.8 copy-start.3
  26.3 0.7 copy-start.4

commit v2 on v0

v2 whole, which is shorter than its diff:
```python
import functools

import jax
import jax.numpy as jnp
from jax import lax
from jax.experimental import pallas as pl
from jax.experimental.pallas import tpu as pltpu
from jax.sharding import PartitionSpec as P

D = 1024
HEADS = 16
HD = 64
BUCKETS = 32

bucket_bounds = (12, 16, 23, 32, 46, 64, 91)
epsilon = 1e-06
MESH = pl.DeviceIdType.MESH
VM = pl.BlockSpec(memory_space=pltpu.VMEM)
ANY = pl.BlockSpec(memory_space=pl.ANY)


def bucket_of(offset):
    distance = jnp.abs(offset)
    far_bucket = jnp.full_like(distance, 8)
    for boundary in bucket_bounds:
        far_bucket = far_bucket + (distance >= boundary).astype(jnp.int32)
    chosen = jnp.where(distance < 8, distance, far_bucket)
    return chosen + 16 * (offset > 0).astype(jnp.int32)


def rms_scale(values, gain):
    mean_square = jnp.mean(values * values, axis=-1, keepdims=True)
    return values * lax.rsqrt(mean_square + epsilon) * gain


def layer_kernel(
    WIDE,
    x_ref, seg_row_ref, seg_col_ref, g1_ref, bias_ref, g2_ref, wq_hbm, wkv_hbm, wo_hbm, win_hbm,
    wout_hbm, out_ref,
    wq, wkv, wo, win, wout, hid, q_scr, kv_scr, att_scr, mid, gath, part, cross, inbox,
    s_load, s_hid, r_hid, s_far, s_near, r_w, s_z, s_y, s_core, r_gath, s_cross, r_cross,
    s_out, r_in,
):
    tok = lax.axis_index("tok")
    blk = lax.axis_index("blk")
    c = lax.rem(blk, 2)
    chip = blk // 2
    y = lax.rem(chip, WIDE)
    z = chip // WIDE
    zp = z + 1 - 2 * lax.rem(z, 2)
    zq = lax.rem(z + 2, 4)
    oc = 1 - c
    n_tok, rows, _ = hid.shape
    count = n_tok * rows
    wide = 2 * count
    half_rows = rows // 2
    piece = win_hbm.shape[0] // n_tok

    def dev(zz, yy, cc):
        return {"blk": (zz * WIDE + yy) * 2 + cc}

    def place(zz, yy):
        return lax.rem(zz, 2) * WIDE + yy

    def beside(d):
        return lax.rem(y + d, WIDE)

    def other_tok(d):
        return lax.rem(tok + d, n_tok)

    def remote(src, dst, ss, rs, to):
        return pltpu.make_async_remote_copy(
            src_ref=src, dst_ref=dst, send_sem=ss, recv_sem=rs, device_id=to, device_id_type=MESH
        )

    sides = range(1, WIDE)
    toks = range(1, n_tok)
    core_dev = dev(z, y, oc)
    near_dev = dev(zp, y, c)
    far_dev = dev(zq, y, c)

    barrier = pltpu.get_barrier_semaphore()
    greet = [core_dev, near_dev, far_dev]
    greet += [dev(z, beside(d), c) for d in sides] + [{"tok": other_tok(d)} for d in toks]
    for to in greet:
        pl.semaphore_signal(barrier, inc=1, device_id=to, device_id_type=MESH)

    loads = [
        pltpu.make_async_copy(src, dst, s_load.at[k])
        for k, (src, dst) in enumerate(
            [(wq_hbm, wq), (wkv_hbm, wkv), (wo_hbm, wo), (win_hbm, win.at[0]), (wout_hbm, wout.at[0])]
        )
    ]
    for load in loads:
        load.start()
    pl.semaphore_wait(barrier, len(greet))

    hid_copies = [
        remote(x_ref, hid.at[tok], s_hid.at[d], r_hid.at[d], {"tok": other_tok(d)}) for d in toks
    ]
    for copy in hid_copies:
        copy.start()

    slices = [(win_hbm, win), (wout_hbm, wout)]
    own_piece = pl.ds(pl.multiple_of(tok * piece, piece), piece)

    def far_copy(k):
        src, dst = slices[k]
        return remote(
            src.at[own_piece], dst.at[1, own_piece], s_far.at[k], r_w.at[k, 0], far_dev
        )

    def near_copy(k, d):
        dst = slices[k][1]
        return remote(
            dst.at[1, own_piece], dst.at[1, own_piece], s_near.at[k, d], r_w.at[k, d],
            {"tok": other_tok(d)},
        )

    for k in range(2):
        far_copy(k).start()

    def share(k):
        far_copy(k).wait_recv()
        for d in toks:
            near_copy(k, d).start()

    hid[tok] = x_ref[...]
    hidden = x_ref[...].astype(jnp.float32)
    normed = rms_scale(hidden, g1_ref[...]).astype(jnp.bfloat16)
    spot = lax.broadcasted_iota(jnp.int32, (BUCKETS, wide), 1)
    offset = jnp.where(spot < count, spot, spot - wide) - tok * rows
    chosen = lax.broadcasted_iota(jnp.int32, (BUCKETS, wide), 0) == bucket_of(offset)
    bias_line = jnp.dot(
        bias_ref[...], chosen.astype(jnp.float32),
        precision=lax.Precision.HIGHEST, preferred_element_type=jnp.float32,
    )
    loads[0].wait()
    q_scr[...] = jnp.dot(normed, wq[...], preferred_element_type=jnp.float32).astype(jnp.bfloat16)
    loads[1].wait()

    def keys_values(values, who):
        kv_scr[pl.ds(pl.multiple_of(who * rows, rows), rows), :] = jnp.dot(
            values, wkv[...], preferred_element_type=jnp.float32
        ).astype(jnp.bfloat16)

    keys_values(normed, tok)
    for d in toks:
        hid_copies[d - 1].wait_recv()
        who = lax.rem(tok + n_tok - d, n_tok)
        keys_values(
            rms_scale(hid[who].astype(jnp.float32), g1_ref[...]).astype(jnp.bfloat16), who
        )
    own_seg = seg_col_ref[pl.ds(pl.multiple_of(tok * rows, rows), rows), :]
    same = own_seg == seg_row_ref[...]
    low = lax.broadcasted_iota(jnp.int32, (rows, 2 * HD), 1) < HD
    for pair in range(HEADS // 2):
        at = pair * 2 * HD
        q_two = q_scr[:, at:at + 2 * HD]
        k_two = kv_scr[:, at:at + 2 * HD]
        v_two = kv_scr[:, D + at:D + at + 2 * HD]
        halves = []
        for half in range(2):
            head = 2 * pair + half
            keep = low if half == 0 else jnp.logical_not(low)
            q_one = jnp.where(keep, q_two, jnp.zeros_like(q_two))
            scores = lax.dot_general(
                q_one, k_two, (((1,), (1,)), ((), ())), preferred_element_type=jnp.float32
            )
            line = jnp.broadcast_to(bias_line[head:head + 1, :], (rows, wide))
            bias = pltpu.roll(line, 0, 1, stride=1, stride_axis=0)[:, :count]
            masked = jnp.where(same, scores + bias, -1e30)
            top = jnp.max(masked, axis=-1, keepdims=True)
            exps = jnp.exp(masked - top)
            total = jnp.sum(exps, axis=-1, keepdims=True)
            mixed = jnp.dot(exps.astype(jnp.bfloat16), v_two, preferred_element_type=jnp.float32)
            halves.append(mixed / total)
        att_scr[:, at:at + 2 * HD] = jnp.where(low, halves[0], halves[1]).astype(jnp.bfloat16)
    loads[2].wait()
    middle = x_ref[...].astype(jnp.float32) + jnp.dot(
        att_scr[...], wo[...], preferred_element_type=jnp.float32
    )
    mid[...] = middle
    own = place(z, y)
    gath[own, c] = rms_scale(middle, g2_ref[...]).astype(jnp.bfloat16)

    def rows_of(half):
        return pl.ds(half * half_rows, half_rows)

    def pass_on(g, half, ss, to):
        spot = gath.at[g, c, rows_of(half)]
        return remote(spot, spot, ss, r_gath.at[g, c, half], to)

    def z_copy(g, half):
        return pass_on(g, half, s_z.at[g, half], near_dev)

    def y_copy(g, half, d):
        return pass_on(g, half, s_y.at[d, g, half], dev(z, beside(d), c))

    def core_copy(g, half):
        return pass_on(g, half, s_core.at[g, half], core_dev)

    def arrived(g, core, half):
        spot = gath.at[g, core, rows_of(half)]
        remote(spot, spot, s_core.at[g, half], r_gath.at[g, core, half], core_dev).wait_recv()

    near = place(zp, y)
    z_copy(own, 0).start()
    for d in sides:
        y_copy(own, 1, d).start()
    z_copy(own, 1).start()
    for d in sides:
        y_copy(own, 0, d).start()
    for half in range(2):
        core_copy(own, half).start()
    share(0)
    arrived(near, c, 0)
    for d in sides:
        y_copy(near, 0, d).start()
    core_copy(near, 0).start()
    for d in sides:
        g = place(z, beside(d))
        arrived(g, c, 1)
        z_copy(g, 1).start()
        core_copy(g, 1).start()
    share(1)
    arrived(near, c, 1)
    core_copy(near, 1).start()
    for d in sides:
        g = place(z, beside(d))
        arrived(g, c, 0)
        core_copy(g, 0).start()

    def cross_copy(g):
        return remote(part.at[g, oc], cross.at[g], s_cross.at[g], r_cross.at[g], core_dev)

    def multiply(g):
        for half in range(2):
            arrived(g, oc, half)
        tokens = gath[g].reshape(2 * rows, D)
        inner = lax.dot_general(
            tokens, win[...].reshape(-1, D), (((1,), (1,)), ((), ())),
            preferred_element_type=jnp.float32,
        )
        inner = jnp.maximum(inner, 0.0).astype(jnp.bfloat16)
        terms = jnp.dot(inner, wout[...].reshape(-1, D), preferred_element_type=jnp.float32)
        part[g] = terms.astype(jnp.bfloat16).reshape(2, rows, D)
        cross_copy(g).start()

    def both_cores(g, half):
        return part[g, c, rows_of(half)].astype(jnp.float32) + cross[g, rows_of(half)].astype(
            jnp.float32
        )

    def send_sum(kind, d, g, half, to):
        return remote(
            part.at[g, c, rows_of(half)], inbox.at[kind, d], s_out.at[kind, d], r_in.at[kind, d], to
        )

    def corner_a(d):
        return send_sum(0, d, place(zp, beside(d)), 0, dev(z, beside(d), c))

    def corner_b(d):
        return send_sum(1, d, place(zp, beside(d)), 1, near_dev)

    def side_a(d):
        return send_sum(2, d, place(z, beside(d)), 0, dev(z, beside(d), c))

    def near_b():
        return send_sum(3, 0, near, 1, near_dev)

    def near_a():
        return send_sum(4, 0, near, 0, near_dev)

    def side_b(d):
        return send_sum(5, d, place(z, beside(d)), 1, dev(z, beside(d), c))

    def got(kind, d):
        send_sum(kind, d, own, 0, core_dev).wait_recv()
        return inbox[kind, d].astype(jnp.float32)

    def settle(g, half, extra):
        part[g, c, rows_of(half)] = (both_cores(g, half) + extra).astype(jnp.bfloat16)

    loads[3].wait()
    loads[4].wait()
    for k in range(2):
        for d in toks:
            near_copy(k, d).wait_recv()
    multiply(own)
    multiply(near)
    for d in sides:
        multiply(place(z, beside(d)))
    cross_copy(near).wait_recv()
    settle(near, 1, 0.0)
    near_b().start()
    for d in sides:
        g = place(zp, beside(d))
        arrived(g, c, 0)
        core_copy(g, 0).start()
        arrived(g, c, 1)
        core_copy(g, 1).start()
    for d in sides:
        g = place(z, beside(d))
        cross_copy(g).wait_recv()
        settle(g, 0, 0.0)
        side_a(d).start()
    for d in sides:
        multiply(place(zp, beside(d)))
    for d in sides:
        g = place(zp, beside(d))
        cross_copy(g).wait_recv()
        settle(g, 0, 0.0)
        corner_a(d).start()
        settle(g, 1, 0.0)
        corner_b(d).start()
    extra = jnp.zeros((half_rows, D), jnp.float32)
    for d in sides:
        extra = extra + got(0, d)
    settle(near, 0, extra)
    near_a().start()
    for d in sides:
        settle(place(z, beside(d)), 1, got(1, d))
        side_b(d).start()
    cross_copy(own).wait_recv()
    for half in range(2):
        at = rows_of(half)
        total = mid[at, :] + both_cores(own, half)
        for d in sides:
            total = total + got((2, 5)[half], d)
        total = total + got((4, 3)[half], 0)
        out_ref[at, :] = total.astype(jnp.bfloat16)

    for copy in hid_copies:
        copy.wait_send()
    for k in range(2):
        far_copy(k).wait_send()
        for d in toks:
            near_copy(k, d).wait_send()
    for half in range(2):
        z_copy(own, half).wait_send()
        for zz in (z, zp):
            for d in range(WIDE):
                core_copy(place(zz, beside(d)), half).wait_send()
    for d in sides:
        y_copy(own, 0, d).wait_send()
        y_copy(own, 1, d).wait_send()
        y_copy(near, 0, d).wait_send()
        z_copy(place(z, beside(d)), 1).wait_send()
        corner_a(d).wait_send()
        corner_b(d).wait_send()
        side_a(d).wait_send()
        side_b(d).wait_send()
    near_a().wait_send()
    near_b().wait_send()
    for zz in (z, zp):
        for d in range(WIDE):
            cross_copy(place(zz, beside(d))).wait_send()


def per_device(
    n_tok, n_blk, hidden_in, seg_ids, norm_gain1, w_query, w_key_value, rel_bias, w_attn_out,
    norm_gain2, w_in, w_out,
):
    rows = hidden_in.shape[1]
    count = n_tok * rows
    units = w_in.shape[0]
    wide = n_blk // 8
    chips = 2 * wide
    dma = pltpu.SemaphoreType.DMA

    def half(*shape):
        return pltpu.VMEM(shape, jnp.bfloat16)

    out = pl.pallas_call(
        functools.partial(layer_kernel, wide),
        out_shape=jax.ShapeDtypeStruct((rows, D), jnp.bfloat16),
        in_specs=[VM] * 6 + [ANY] * 5,
        out_specs=VM,
        scratch_shapes=[
            half(D, D),
            half(D, 2 * D),
            half(D, D),
            half(2, units, D),
            half(2, units, D),
            half(n_tok, rows, D),
            half(rows, D),
            half(count, 2 * D),
            half(rows, D),
            pltpu.VMEM((rows, D), jnp.float32),
            half(chips, 2, rows, D),
            half(chips, 2, rows, D),
            half(chips, rows, D),
            half(6, wide, rows // 2, D),
            dma((5,)),
            dma((n_tok,)),
            dma((n_tok,)),
            dma((2,)),
            dma((2, n_tok)),
            dma((2, n_tok)),
            dma((chips, 2)),
            dma((wide, chips, 2)),
            dma((chips, 2)),
            dma((chips, 2, 2)),
            dma((chips,)),
            dma((chips,)),
            dma((6, wide)),
            dma((6, wide)),
        ],
        compiler_params=pltpu.CompilerParams(
            collective_id=0, has_side_effects=True, vmem_limit_bytes=60 << 20
        ),
    )(
        hidden_in[0], seg_ids, jnp.transpose(seg_ids), norm_gain1[None], jnp.transpose(rel_bias),
        norm_gain2[None], w_query, w_key_value, w_attn_out, w_in, w_out,
    )
    return out[None]


def solution(mesh):
    placed = (
        P("blk", "tok", None),
        P("blk", None),
        P(),
        P(),
        P(),
        P(),
        P(),
        P(),
        P("blk", None),
        P("blk", None),
    )
    return jax.shard_map(
        functools.partial(per_device, mesh.shape["tok"], mesh.shape["blk"]),
        mesh=mesh, in_specs=placed, out_specs=P("blk", "tok", None), check_vma=False,
    )
```

time: 289 us -> 58.3 us (0.20)
  waiting for transfers between devices: 125 us -> 0 us
  local copies, waits for them, and re-layouts: 124 us -> 3.14 us
  Pallas kernels: 0 us -> 55 us
  matrix products: 19.2 us -> 0 us
  between operations: 13.2 us -> 0.01 us
  other arithmetic: 6.67 us -> 0 us
    gather x2 -> x0, local copies, waits for them, and re-layouts: 120 us -> none  [per_device(): jnp.take(bias_table, bucket_of(offsets), axis=1)]
    reduce_scatter x1 -> x0, waiting for transfers between devices: 71.3 us -> none  [per_device(): lax.psum_scatter(terms.astype(jnp.bfloat16), 'blk', scatter_dimension=0,...]
    pallas_call x0 -> x1, Pallas kernels: none -> 55 us  [per_device(): pl.pallas_call(functools.partial(layer_kernel, wide), out_shape=jax.Shape...]
    all_gather x2 -> x0, waiting for transfers between devices: 53.4 us -> none  [the longest x1 53.4 us: per_device(): lax.all_gather(normed_two, 'blk', axis=0, tiled=True)]
    dot_general x6 -> x0, matrix products: 19.2 us -> none  [the longest x1 8.51 us: per_device(): jnp.dot(inner, w_out, preferred_element_type=jnp.float32)]
    reduce_sum x2 -> x0, other arithmetic: 3.64 us -> none  [the longest x1 2.41 us: per_device(): new_sum = jnp.sum(exps, axis=-1)]
    slice x3 -> x0, local copies, waits for them, and re-layouts: 3.5 us -> none  [the longest x2 3.3 us: per_device(): key_heads = attend_keys_values[:, :D].reshape(count, HEADS, HD)]
  transfers between devices with their start and end apart: 3 -> 0, of which waited for: 2 -> 0; matrix products, arithmetic and copies ran while one was open for 43% -> 0% of each run, Pallas kernels for 0% -> 0%
where the time goes in v2:
time: 58.3 us; the launch traced here: 58.2 us
  Pallas kernels  55 us (94%)
  local copies, waits for them, and re-layouts  3.14 us (5%)
    pallas_call x1, Pallas kernels, per_device(): pl.pallas_call(functools.partial(layer_kernel, wide), out_shape=jax.Shape...  55 us
    unnamed x1, local copies, waits for them, and re-layouts  1.67 us
    transpose x1, local copies, waits for them, and re-layouts, per_device(): jnp.transpose(seg_ids)  1.47 us

profile of v2, /device:TPU:0, one launch (start us, length us, event | category | flops | bytes accessed | tf_op | source)
XLA Modules:
  0.0 58.2 jit_solution(359093486177625607)
XLA Ops:
  0.0 1.5 %copy.11.seg_col_ref = s32[256,1]{1,0:T(8,128)} copy(s32[256,1]{0,1:T(1,128)} %bitcast.11) | data formatting | bytes 2048 | tf_op jit(solution)/shard_map/transpose | solution.py:414
  1.5 55.0 %shard_map.100 = bf16[128,1024]{1,0:T(8,128)(2,1)} custom-call(bf16[128,1024]{1,0:T(8,128)(2,1)} %bitcast.7, s32[1,256]{1,0:T(1,128)} %seg_row_ref.1, s32[256,1]{1,0:T(8,128)} %copy.11.seg_col_ref, f32[1,1024]{1,0:T(1,128)} %bitcast.9, f32[16,32]{1,0:T(8,128)} %bitcast.8, f32[1,1024]{1,0:T(1,128)} %bitcast.10, bf16[1024,1024]{1,0:T(8,128)(2,1)} %wq_hbm.1, ...), custom_call_target="tpu_custom_call" | custom-call | tf_op jit(solution)/shard_map/pallas_call | solution.py:375
  56.5 1.7 %copy.13 = bf16[1,128,1024]{2,1,0:T(8,128)(2,1)} copy(bf16[1,128,1024]{2,1,0:T(8,128)(2,1)} %bitcast.6) | data formatting | bytes 524288

commit v3 on v2

--- a/solution.py
+++ b/solution.py
@@ -35,9 +35,9 @@
 
 def layer_kernel(
     WIDE,
-    x_ref, seg_row_ref, seg_col_ref, g1_ref, bias_ref, g2_ref, wq_hbm, wkv_hbm, wo_hbm, win_hbm,
+    x_ref, seg_row_ref, g1_ref, bias_ref, g2_ref, wq_hbm, wkv_hbm, wo_hbm, win_hbm,
     wout_hbm, out_ref,
-    wq, wkv, wo, win, wout, hid, q_scr, kv_scr, att_scr, mid, gath, part, cross, inbox,
+    wq, wkv, wo, win, wout, hid, q_scr, kv_scr, att_scr, mid, gath, part, cross, inbox, inner_scr,
     s_load, s_hid, r_hid, s_far, s_near, r_w, s_z, s_y, s_core, r_gath, s_cross, r_cross,
     s_out, r_in,
 ):
@@ -102,28 +102,36 @@
         copy.start()
 
     slices = [(win_hbm, win), (wout_hbm, wout)]
-    own_piece = pl.ds(pl.multiple_of(tok * piece, piece), piece)
-
-    def far_copy(k):
+    part_rows = piece // 2
+
+    def spot_of(half):
+        return pl.ds(pl.multiple_of(tok * piece + half * part_rows, part_rows), part_rows)
+
+    def far_copy(k, half):
         src, dst = slices[k]
         return remote(
-            src.at[own_piece], dst.at[1, own_piece], s_far.at[k], r_w.at[k, 0], far_dev
-        )
-
-    def near_copy(k, d):
-        dst = slices[k][1]
+            src.at[spot_of(half)], dst.at[1, spot_of(half)], s_far.at[k, half],
+            r_w.at[k, half, 0], far_dev,
+        )
+
+    def near_copy(k, half, d):
+        spot = slices[k][1].at[1, spot_of(half)]
         return remote(
-            dst.at[1, own_piece], dst.at[1, own_piece], s_near.at[k, d], r_w.at[k, d],
-            {"tok": other_tok(d)},
-        )
-
-    for k in range(2):
-        far_copy(k).start()
-
-    def share(k):
-        far_copy(k).wait_recv()
+            spot, spot, s_near.at[k, half, d], r_w.at[k, half, d], {"tok": other_tok(d)}
+        )
+
+    for half in range(2):
+        far_copy(0, half).start()
+
+    def share(k, half):
+        far_copy(k, half).wait_recv()
         for d in toks:
-            near_copy(k, d).start()
+            near_copy(k, half, d).start()
+
+    def shared(k):
+        for half in range(2):
+            for d in toks:
+                near_copy(k, half, d).wait_recv()
 
     hid[tok] = x_ref[...]
     hidden = x_ref[...].astype(jnp.float32)
@@ -151,8 +159,13 @@
         keys_values(
             rms_scale(hid[who].astype(jnp.float32), g1_ref[...]).astype(jnp.bfloat16), who
         )
-    own_seg = seg_col_ref[pl.ds(pl.multiple_of(tok * rows, rows), rows), :]
-    same = own_seg == seg_row_ref[...]
+    seg_row = jnp.broadcast_to(seg_row_ref[...].astype(jnp.float32), (rows, count))
+    diagonal = lax.broadcasted_iota(jnp.int32, (rows, count), 1) == tok * rows + (
+        lax.broadcasted_iota(jnp.int32, (rows, count), 0)
+    )
+    same = jnp.sum(jnp.where(diagonal, seg_row, 0.0), axis=-1, keepdims=True) == seg_row
+    for half in range(2):
+        far_copy(1, half).start()
     low = lax.broadcasted_iota(jnp.int32, (rows, 2 * HD), 1) < HD
     for pair in range(HEADS // 2):
         at = pair * 2 * HD
@@ -204,7 +217,67 @@
         spot = gath.at[g, core, rows_of(half)]
         remote(spot, spot, s_core.at[g, half], r_gath.at[g, core, half], core_dev).wait_recv()
 
+    def first(g, k):
+        tokens = gath[g].reshape(2 * rows, D)
+        units = win.shape[1]
+        inner = lax.dot_general(
+            tokens, win[k], (((1,), (1,)), ((), ())), preferred_element_type=jnp.float32
+        )
+        inner_scr[g, :, k * units:(k + 1) * units] = jnp.maximum(inner, 0.0).astype(jnp.bfloat16)
+
+    def begin(g):
+        for half in range(2):
+            arrived(g, oc, half)
+        first(g, 0)
+
+    def cross_copy(g):
+        return remote(part.at[g, oc], cross.at[g], s_cross.at[g], r_cross.at[g], core_dev)
+
+    def second(g):
+        terms = jnp.dot(
+            inner_scr[g], wout[...].reshape(-1, D), preferred_element_type=jnp.float32
+        )
+        part[g] = terms.astype(jnp.bfloat16).reshape(2, rows, D)
+        cross_copy(g).start()
+
+    def both_cores(g, half):
+        return part[g, c, rows_of(half)].astype(jnp.float32) + cross[g, rows_of(half)].astype(
+            jnp.float32
+        )
+
+    def send_sum(kind, d, g, half, to):
+        return remote(
+            part.at[g, c, rows_of(half)], inbox.at[kind, d], s_out.at[kind, d], r_in.at[kind, d], to
+        )
+
+    def corner_a(d):
+        return send_sum(0, d, place(zp, beside(d)), 0, dev(z, beside(d), c))
+
+    def corner_b(d):
+        return send_sum(1, d, place(zp, beside(d)), 1, near_dev)
+
+    def side_a(d):
+        return send_sum(2, d, place(z, beside(d)), 0, dev(z, beside(d), c))
+
+    def near_b():
+        return send_sum(3, 0, near, 1, near_dev)
+
+    def near_a():
+        return send_sum(4, 0, near, 0, near_dev)
+
+    def side_b(d):
+        return send_sum(5, d, place(z, beside(d)), 1, dev(z, beside(d), c))
+
+    def got(kind, d):
+        send_sum(kind, d, own, 0, core_dev).wait_recv()
+        return inbox[kind, d].astype(jnp.float32)
+
+    def settle(g, half, extra):
+        part[g, c, rows_of(half)] = (both_cores(g, half) + extra).astype(jnp.bfloat16)
+
     near = place(zp, y)
+    side_chips = [place(z, beside(d)) for d in sides]
+    corners = [place(zp, beside(d)) for d in sides]
     z_copy(own, 0).start()
     for d in sides:
         y_copy(own, 1, d).start()
@@ -213,107 +286,63 @@
         y_copy(own, 0, d).start()
     for half in range(2):
         core_copy(own, half).start()
-    share(0)
+    loads[3].wait()
+    begin(own)
+    share(0, 0)
     arrived(near, c, 0)
     for d in sides:
         y_copy(near, 0, d).start()
     core_copy(near, 0).start()
-    for d in sides:
-        g = place(z, beside(d))
+    for g in side_chips:
         arrived(g, c, 1)
         z_copy(g, 1).start()
         core_copy(g, 1).start()
-    share(1)
+    share(0, 1)
     arrived(near, c, 1)
     core_copy(near, 1).start()
-    for d in sides:
-        g = place(z, beside(d))
+    for g in side_chips:
         arrived(g, c, 0)
         core_copy(g, 0).start()
-
-    def cross_copy(g):
-        return remote(part.at[g, oc], cross.at[g], s_cross.at[g], r_cross.at[g], core_dev)
-
-    def multiply(g):
+    share(1, 0)
+    begin(near)
+    for g in side_chips:
+        begin(g)
+    share(1, 1)
+    for g in corners:
         for half in range(2):
-            arrived(g, oc, half)
-        tokens = gath[g].reshape(2 * rows, D)
-        inner = lax.dot_general(
-            tokens, win[...].reshape(-1, D), (((1,), (1,)), ((), ())),
-            preferred_element_type=jnp.float32,
-        )
-        inner = jnp.maximum(inner, 0.0).astype(jnp.bfloat16)
-        terms = jnp.dot(inner, wout[...].reshape(-1, D), preferred_element_type=jnp.float32)
-        part[g] = terms.astype(jnp.bfloat16).reshape(2, rows, D)
-        cross_copy(g).start()
-
-    def both_cores(g, half):
-        return part[g, c, rows_of(half)].astype(jnp.float32) + cross[g, rows_of(half)].astype(
-            jnp.float32
-        )
-
-    def send_sum(kind, d, g, half, to):
-        return remote(
-            part.at[g, c, rows_of(half)], inbox.at[kind, d], s_out.at[kind, d], r_in.at[kind, d], to
-        )
-
-    def corner_a(d):
-        return send_sum(0, d, place(zp, beside(d)), 0, dev(z, beside(d), c))
-
-    def corner_b(d):
-        return send_sum(1, d, place(zp, beside(d)), 1, near_dev)
-
-    def side_a(d):
-        return send_sum(2, d, place(z, beside(d)), 0, dev(z, beside(d), c))
-
-    def near_b():
-        return send_sum(3, 0, near, 1, near_dev)
-
-    def near_a():
-        return send_sum(4, 0, near, 0, near_dev)
-
-    def side_b(d):
-        return send_sum(5, d, place(z, beside(d)), 1, dev(z, beside(d), c))
-
-    def got(kind, d):
-        send_sum(kind, d, own, 0, core_dev).wait_recv()
-        return inbox[kind, d].astype(jnp.float32)
-
-    def settle(g, half, extra):
-        part[g, c, rows_of(half)] = (both_cores(g, half) + extra).astype(jnp.bfloat16)
-
-    loads[3].wait()
+            arrived(g, c, half)
+            core_copy(g, half).start()
+    shared(0)
+    first(near, 1)
+    for g in side_chips:
+        first(g, 1)
+    for g in corners:
+        begin(g)
+        first(g, 1)
     loads[4].wait()
-    for k in range(2):
-        for d in toks:
-            near_copy(k, d).wait_recv()
-    multiply(own)
-    multiply(near)
-    for d in sides:
-        multiply(place(z, beside(d)))
-    cross_copy(near).wait_recv()
-    settle(near, 1, 0.0)
-    near_b().start()
-    for d in sides:
-        g = place(zp, beside(d))
-        arrived(g, c, 0)
-        core_copy(g, 0).start()
-        arrived(g, c, 1)
-        core_copy(g, 1).start()
-    for d in sides:
-        g = place(z, beside(d))
-        cross_copy(g).wait_recv()
-        settle(g, 0, 0.0)
-        side_a(d).start()
-    for d in sides:
-        multiply(place(zp, beside(d)))
-    for d in sides:
-        g = place(zp, beside(d))
+    shared(1)
+    for g in corners:
+        second(g)
+    second(near)
+    for d in sides:
+        g = corners[d - 1]
         cross_copy(g).wait_recv()
         settle(g, 0, 0.0)
         corner_a(d).start()
         settle(g, 1, 0.0)
         corner_b(d).start()
+    for g in side_chips:
+        second(g)
+    cross_copy(near).wait_recv()
+    settle(near, 1, 0.0)
+    near_b().start()
+    for d in sides:
+        g = side_chips[d - 1]
+        cross_copy(g).wait_recv()
+        settle(g, 0, 0.0)
+        side_a(d).start()
+    first(own, 1)
+    second(own)
     extra = jnp.zeros((half_rows, D), jnp.float32)
     for d in sides:
         extra = extra + got(0, d)
@@ -334,9 +363,10 @@
     for copy in hid_copies:
         copy.wait_send()
     for k in range(2):
-        far_copy(k).wait_send()
-        for d in toks:
-            near_copy(k, d).wait_send()
+        for half in range(2):
+            far_copy(k, half).wait_send()
+            for d in toks:
+                near_copy(k, half, d).wait_send()
     for half in range(2):
         z_copy(own, half).wait_send()
         for zz in (z, zp):
@@ -375,7 +405,7 @@
     out = pl.pallas_call(
         functools.partial(layer_kernel, wide),
         out_shape=jax.ShapeDtypeStruct((rows, D), jnp.bfloat16),
-        in_specs=[VM] * 6 + [ANY] * 5,
+        in_specs=[VM] * 5 + [ANY] * 5,
         out_specs=VM,
         scratch_shapes=[
             half(D, D),
@@ -392,12 +422,13 @@
             half(chips, 2, rows, D),
             half(chips, rows, D),
             half(6, wide, rows // 2, D),
+            half(chips, 2 * rows, 2 * units),
             dma((5,)),
             dma((n_tok,)),
             dma((n_tok,)),
-            dma((2,)),
-            dma((2, n_tok)),
-            dma((2, n_tok)),
+            dma((2, 2)),
+            dma((2, 2, n_tok)),
+            dma((2, 2, n_tok)),
             dma((chips, 2)),
             dma((wide, chips, 2)),
             dma((chips, 2)),
@@ -411,7 +442,7 @@
             collective_id=0, has_side_effects=True, vmem_limit_bytes=60 << 20
         ),
     )(
-        hidden_in[0], seg_ids, jnp.transpose(seg_ids), norm_gain1[None], jnp.transpose(rel_bias),
+        hidden_in[0], seg_ids, norm_gain1[None], jnp.transpose(rel_bias),
         norm_gain2[None], w_query, w_key_value, w_attn_out, w_in, w_out,
     )
     return out[None]

time: 58.3 us -> 56.2 us (0.964)
  local copies, waits for them, and re-layouts: 3.14 us -> 1.67 us
  Pallas kernels: 55 us -> 54.3 us
    transpose x1 -> x0, local copies, waits for them, and re-layouts: 1.47 us -> none  [per_device(): jnp.transpose(seg_ids)]
    pallas_call x1, Pallas kernels: 55 us -> 54.3 us  [per_device(): pl.pallas_call(functools.partial(layer_kernel, wide), out_shape=jax.Shape...]
where the time goes in v3:
time: 56.2 us; the launch traced here: 56 us
  Pallas kernels  54.3 us (97%)
  local copies, waits for them, and re-layouts  1.67 us (3%)
    pallas_call x1, Pallas kernels, per_device(): pl.pallas_call(functools.partial(layer_kernel, wide), out_shape=jax.Shape...  54.3 us
    unnamed x1, local copies, waits for them, and re-layouts  1.67 us

profile of v3, /device:TPU:0, one launch (start us, length us, event | category | flops | bytes accessed | tf_op | source)
XLA Modules:
  0.0 56.0 jit_solution(4842312939914812178)
XLA Ops:
  0.0 54.3 %shard_map.100 = bf16[128,1024]{1,0:T(8,128)(2,1)} custom-call(bf16[128,1024]{1,0:T(8,128)(2,1)} %bitcast.6, s32[1,256]{1,0:T(1,128)} %seg_row_ref.1, f32[1,1024]{1,0:T(1,128)} %bitcast.8, f32[16,32]{1,0:T(8,128)} %bitcast.7, f32[1,1024]{1,0:T(1,128)} %bitcast.9, bf16[1024,1024]{1,0:T(8,128)(2,1)} %wq_hbm.1, bf16[1024,2048]{1,0:T(8,128)(2,1)} %wkv_hbm.1, ...), custom_call_target="tpu_custom_call" | custom-call | tf_op jit(solution)/shard_map/pallas_call | solution.py:405
  54.3 1.7 %copy.12 = bf16[1,128,1024]{2,1,0:T(8,128)(2,1)} copy(bf16[1,128,1024]{2,1,0:T(8,128)(2,1)} %bitcast.5) | data formatting | bytes 524288

commit v4 on v3

--- a/solution.py
+++ b/solution.py
@@ -120,8 +120,9 @@
             spot, spot, s_near.at[k, half, d], r_w.at[k, half, d], {"tok": other_tok(d)}
         )
 
-    for half in range(2):
-        far_copy(0, half).start()
+    for k in range(2):
+        for half in range(2):
+            far_copy(k, half).start()
 
     def share(k, half):
         far_copy(k, half).wait_recv()
@@ -164,8 +165,6 @@
         lax.broadcasted_iota(jnp.int32, (rows, count), 0)
     )
     same = jnp.sum(jnp.where(diagonal, seg_row, 0.0), axis=-1, keepdims=True) == seg_row
-    for half in range(2):
-        far_copy(1, half).start()
     low = lax.broadcasted_iota(jnp.int32, (rows, 2 * HD), 1) < HD
     for pair in range(HEADS // 2):
         at = pair * 2 * HD

time: 56.2 us -> 58.2 us (1.036)
  Pallas kernels: 54.3 us -> 56.4 us
    pallas_call x1, Pallas kernels: 54.3 us -> 56.4 us  [per_device(): pl.pallas_call(functools.partial(layer_kernel, wide), out_shape=jax.Shape...]
where the time goes in v4:
time: 58.2 us; the launch traced here: 58 us
  Pallas kernels  56.4 us (97%)
  local copies, waits for them, and re-layouts  1.67 us (3%)
    pallas_call x1, Pallas kernels, per_device(): pl.pallas_call(functools.partial(layer_kernel, wide), out_shape=jax.Shape...  56.4 us
    unnamed x1, local copies, waits for them, and re-layouts  1.67 us

profile of v4, /device:TPU:0, one launch (start us, length us, event | category | flops | bytes accessed | tf_op | source)
XLA Modules:
  0.0 58.0 jit_solution(16881435954493252625)
XLA Ops:
  0.0 56.4 %shard_map.100 = bf16[128,1024]{1,0:T(8,128)(2,1)} custom-call(bf16[128,1024]{1,0:T(8,128)(2,1)} %bitcast.6, s32[1,256]{1,0:T(1,128)} %seg_row_ref.1, f32[1,1024]{1,0:T(1,128)} %bitcast.8, f32[16,32]{1,0:T(8,128)} %bitcast.7, f32[1,1024]{1,0:T(1,128)} %bitcast.9, bf16[1024,1024]{1,0:T(8,128)(2,1)} %wq_hbm.1, bf16[1024,2048]{1,0:T(8,128)(2,1)} %wkv_hbm.1, ...), custom_call_target="tpu_custom_call" | custom-call | tf_op jit(solution)/shard_map/pallas_call | solution.py:404
  56.4 1.7 %copy.12 = bf16[1,128,1024]{2,1,0:T(8,128)(2,1)} copy(bf16[1,128,1024]{2,1,0:T(8,128)(2,1)} %bitcast.5) | data formatting | bytes 524288
